TPU v7x, 32 devices: a whole 2x2x4 slice. The times are simulated.
32 devices in a mesh: row: 4 (over y, core), col: 8 (over z, x).
Axes of the slice: x: 2, y: 2, z: 4, core: 2. Of those that a mesh axis runs over, the one named last changes fastest.
Arguments:
- inputs: bfloat16 [512, 12288], P('col', 'row'), may hold values from -6 to 6
- grad_out: bfloat16 [512, 12288], P('col', 'row'), may hold values from -6 to 6
- w_in: bfloat16 [12288, 24576], P('row', 'col'), may hold values from -0.0546875 to 0.0546875
- w_out: bfloat16 [24576, 12288], P('col', 'row'), may hold values from -0.0390625 to 0.0390625
Outputs:
- outputs: bfloat16 [512, 12288], P('col', 'row')
- grad_in: bfloat16 [512, 12288], P('col', 'row')
- grad_w_in: bfloat16 [12288, 24576], P('row', 'col')
- grad_w_out: bfloat16 [24576, 12288], P('col', 'row')
All inputs are finite; a program needn't handle non-finite values.
Results may differ from a plain program's by a relative error of at most 0.019.
Values may be sent and summed in bfloat16 or wider, within the bound.
A program may use at most 192 MiB of HBM per device.

v0:
```python
from functools import partial
import jax
import jax.numpy as jnp
from jax import lax
from jax.sharding import PartitionSpec as P


def col_panel(values):
    return lax.all_gather(values, "col", axis=0, tiled=True)


def contract(left, right, dims):
    return lax.dot_general(
        left, right, ((dims[0], dims[1]), ((), ())), preferred_element_type=jnp.float32
    )


def row_sums(left, right, dims):
    return lax.psum_scatter(
        contract(left, right, dims).astype(jnp.bfloat16), "row", scatter_dimension=0, tiled=True
    ).astype(jnp.float32)


def row_spread(values):
    return lax.all_gather(values, "row", axis=0, tiled=True)


def col_sums(left, right, dims):
    return lax.psum_scatter(
        contract(
            lax.dynamic_slice_in_dim(
                left, jnp.int32(0), left.shape[0] // lax.axis_size("col") * lax.axis_size("col"), 0
            ),
            right,
            dims,
        ).astype(jnp.bfloat16),
        "col",
        scatter_dimension=0,
        tiled=True,
    ).astype(jnp.float32)


def local(inputs, grad_out, w_in, w_out):
    gelu_tanh = partial(jax.nn.gelu, approximate=True)
    input_all = col_panel(inputs)
    cotan_all = None
    hidden_pre = row_sums(input_all, w_in, ((1,), (0,)))
    act_all = row_spread(gelu_tanh(hidden_pre).astype(jnp.bfloat16))
    outputs = col_sums(act_all, w_out, ((1,), (0,))).astype(jnp.bfloat16)
    cotan_all = col_panel(grad_out)
    grad_act = row_sums(cotan_all, w_out, ((1,), (1,)))
    grad_pre = jax.vjp(gelu_tanh, hidden_pre)[1](grad_act)[0].astype(jnp.bfloat16)
    grad_pre_all = row_spread(grad_pre)
    grad_w_out = contract(act_all, cotan_all, ((0,), (0,))).astype(jnp.bfloat16)
    grad_w_in = contract(input_all, grad_pre_all, ((0,), (0,))).astype(jnp.bfloat16)
    grad_in = col_sums(grad_pre_all, w_in, ((1,), (1,))).astype(jnp.bfloat16)
    return (outputs, grad_in, grad_w_in, grad_w_out)


def solution(mesh):
    placed = (P("col", "row"), P("col", "row"), P("row", "col"), P("col", "row"))
    return jax.shard_map(
        local,
        mesh=mesh,
        in_specs=placed,
        out_specs=(P("col", "row"), P("col", "row"), P("row", "col"), P("col", "row")),
        check_vma=False,
    )
```

profile of v0, /device:TPU:0, one launch (start us, length us, event | category | flops | bytes accessed | tf_op | source)
XLA Modules:
  0.0 441.4 jit_solution(10468758725500619523)
XLA Ops:
  7.2 0.0 all-gather.9.cloned.1.call-start
  7.2 0.7 all-gather.9.cloned.1.call-update
  7.9 0.0 all-gather.5.cloned.1.call-start
  7.9 0.7 all-gather.5.cloned.1.call-update
  8.6 0.0 reduce-scatter.9.cloned.1.call-start
  8.7 64.7 %all-gather.9.cloned.1.call-done = bf16[512,3072]{1,0:T(8,128)(2,1)} async-done(((bf16[64,3072]{1,0:T(8,128)(2,1)}), bf16[512,3072]{1,0:T(8,128)(2,1)}) %all-gather.9.cloned.1.call-update) | async-done | bytes 3145744 | tf_op jit(solution)/shard_map/all_gather | solution.py:9
  73.4 15.9 %convolution_convert_fusion.2 = bf16[512,3072]{1,0:T(8,128)(2,1)} fusion(bf16[512,3072]{1,0:T(8,128)(2,1)} %all-gather.9.cloned.1.call-done, bf16[3072,3072]{1,0:T(8,128)(2,1)} %param.7), kind=kOutput, calls=%fused_computation.3 | convolution fusion | flops 9665249280 | bytes 25165824 | tf_op jit(solution)/shard_map/dot_general | solution.py:13
  89.2 0.0 reduce-scatter.9.cloned.1.call-update
  89.3 0.0 reduce-scatter.5.cloned.1.call-start
  89.3 45.4 %all-gather.5.cloned.1.call-done = bf16[512,3072]{1,0:T(8,128)(2,1)} async-done(((bf16[64,3072]{1,0:T(8,128)(2,1)}), bf16[512,3072]{1,0:T(8,128)(2,1)}) %all-gather.5.cloned.1.call-update) | async-done | bytes 3145744 | tf_op jit(solution)/shard_map/all_gather | solution.py:9
  134.7 15.8 %convolution_convert_fusion.4 = bf16[512,3072]{1,0:T(8,128)(2,1)} fusion(bf16[512,3072]{1,0:T(8,128)(2,1)} %all-gather.5.cloned.1.call-done, bf16[3072,3072]{1,0:T(8,128)(2,1)} %param.6), kind=kOutput, calls=%fused_computation.5 | convolution fusion | flops 9665249280 | bytes 25165824 | tf_op jit(solution)/shard_map/dot_general | solution.py:13
  150.4 0.0 reduce-scatter.5.cloned.1.call-update
  150.5 0.0 all-gather.7.cloned.1.call-start
  150.5 23.9 %reduce-scatter.9.cloned.1.call-done = bf16[128,3072]{1,0:T(8,128)(2,1)} async-done(((bf16[512,3072]{1,0:T(8,128)(2,1)}), bf16[128,3072]{1,0:T(8,128)(2,1)}) %reduce-scatter.9.cloned.1.call-update) | async-done | bytes 786448 | tf_op jit(solution)/shard_map/reduce_scatter | solution.py:19
  174.4 41.1 %reduce-scatter.5.cloned.1.call-done = bf16[128,3072]{1,0:T(8,128)(2,1)} async-done(((bf16[512,3072]{1,0:T(8,128)(2,1)}), bf16[128,3072]{1,0:T(8,128)(2,1)}) %reduce-scatter.5.cloned.1.call-update) | async-done | bytes 786448 | tf_op jit(solution)/shard_map/reduce_scatter | solution.py:19
  215.5 3.7 fusion.3
  219.2 0.0 all-gather.7.cloned.1.call-update
  219.3 0.0 all-gather.11.cloned.1.call-start
  219.3 0.5 all-gather.11.cloned.1.call-update
  219.8 0.0 reduce-scatter.7.cloned.1.call-start
  219.9 28.1 %all-gather.7.cloned.1.call-done = bf16[512,3072]{1,0:T(8,128)(2,1)} async-done(((bf16[128,3072]{1,0:T(8,128)(2,1)}), bf16[512,3072]{1,0:T(8,128)(2,1)}) %all-gather.7.cloned.1.call-update) | async-done | bytes 3145744 | tf_op jit(solution)/shard_map/all_gather | solution.py:25
  248.0 15.8 %convolution_convert_fusion.3 = bf16[512,3072]{1,0:T(8,128)(2,1)} fusion(bf16[512,3072]{1,0:T(8,128)(2,1)} %all-gather.7.cloned.1.call-done, bf16[3072,3072]{1,0:T(8,128)(2,1)} %param.7), kind=kOutput, calls=%fused_computation.4 | convolution fusion | flops 9665249280 | bytes 25165824 | tf_op jit(solution)/shard_map/dot_general | solution.py:13
  263.8 0.0 reduce-scatter.7.cloned.1.call-update
  263.8 0.2 reduce-scatter.11.cloned.1.call-start
  264.0 14.5 %all-gather.11.cloned.1.call-done = bf16[512,3072]{1,0:T(8,128)(2,1)} async-done(((bf16[128,3072]{1,0:T(8,128)(2,1)}), bf16[512,3072]{1,0:T(8,128)(2,1)}) %all-gather.11.cloned.1.call-update) | async-done | bytes 3145744 | tf_op jit(solution)/shard_map/all_gather | solution.py:25
  278.5 15.9 %convolution_convert_fusion.1 = bf16[512,3072]{1,0:T(8,128)(2,1)} fusion(bf16[512,3072]{1,0:T(8,128)(2,1)} %all-gather.11.cloned.1.call-done, bf16[3072,3072]{1,0:T(8,128)(2,1)} %param.6), kind=kOutput, calls=%fused_computation.2 | convolution fusion | flops 9665249280 | bytes 25165824 | tf_op jit(solution)/shard_map/dot_general | solution.py:13
  294.5 1.9 copy-done.1
  296.4 15.1 %convert_bitcast_fusion = bf16[3072,3072]{0,1:T(8,128)(2,1)} fusion(bf16[512,3072]{1,0:T(8,128)(2,1)} %all-gather.11.cloned.1.call-done, bf16[512,3072]{1,0:T(8,128)(2,1)S(1)} %copy-done.1), kind=kOutput, calls=%fused_computation | convolution fusion | flops 9673113600 | bytes 25165824 | tf_op jit(solution)/shard_map/dot_general | solution.py:13
  311.5 24.8 %copy.8 = bf16[3072,3072]{1,0:T(8,128)(2,1)} copy(bf16[3072,3072]{0,1:T(8,128)(2,1)} %convert_bitcast_fusion) | data formatting | bytes 37748736
  336.3 15.0 %convolution_convert_fusion = bf16[3072,3072]{1,0:T(8,128)(2,1)} fusion(bf16[512,3072]{1,0:T(8,128)(2,1)} %all-gather.7.cloned.1.call-done, bf16[512,3072]{1,0:T(8,128)(2,1)S(1)} %copy-done), kind=kOutput, calls=%fused_computation.1 | convolution fusion | flops 9673113600 | bytes 25165824 | tf_op jit(solution)/shard_map/dot_general | solution.py:13
  351.3 5.6 %reduce-scatter.7.cloned.1.call-done = bf16[64,3072]{1,0:T(8,128)(2,1)} async-done(((bf16[512,3072]{1,0:T(8,128)(2,1)}), bf16[64,3072]{1,0:T(8,128)(2,1)}) %reduce-scatter.7.cloned.1.call-update) | async-done | bytes 393232 | tf_op jit(solution)/shard_map/reduce_scatter | solution.py:29
  356.9 77.6 %reduce-scatter.11.cloned.1.call-done = bf16[64,3072]{1,0:T(8,128)(2,1)} async-done(((bf16[512,3072]{1,0:T(8,128)(2,1)}), bf16[64,3072]{1,0:T(8,128)(2,1)}) %reduce-scatter.11.cloned.1.call-update) | async-done | bytes 393232 | tf_op jit(solution)/shard_map/reduce_scatter | solution.py:29
  (4 shorter events, 0.0 us)
Async XLA Ops:
  7.2 66.2 %all-gather.9.cloned.1.call-start = ((), (), s32[]{:S(2)}) async-start(), calls=%async_computation.8 | async-start | bytes 3538944 | tf_op jit(solution)/shard_map/all_gather | solution.py:9
  7.9 126.8 %all-gather.5.cloned.1.call-start = ((), (), s32[]{:S(2)}) async-start(), calls=%async_computation.4 | async-start | bytes 3538944 | tf_op jit(solution)/shard_map/all_gather | solution.py:9
  8.6 165.7 %reduce-scatter.9.cloned.1.call-start = ((), (), s32[]{:S(2)}) async-start(), calls=%async_computation.9 | async-start | bytes 3932160 | tf_op jit(solution)/shard_map/reduce_scatter | solution.py:19
  89.3 126.2 %reduce-scatter.5.cloned.1.call-start = ((), (), s32[]{:S(2)}) async-start(), calls=%async_computation.5 | async-start | bytes 3932160 | tf_op jit(solution)/shard_map/reduce_scatter | solution.py:19
  150.5 97.5 %all-gather.7.cloned.1.call-start = ((), (), s32[]{:S(2)}) async-start(), calls=%async_computation.6 | async-start | bytes 3932160 | tf_op jit(solution)/shard_map/all_gather | solution.py:25
  219.3 59.3 %all-gather.11.cloned.1.call-start = ((), (), s32[]{:S(2)}) async-start(), calls=%async_computation.10 | async-start | bytes 3932160 | tf_op jit(solution)/shard_map/all_gather | solution.py:25
  219.8 137.1 %reduce-scatter.7.cloned.1.call-start = ((), (), s32[]{:S(2)}) async-start(), calls=%async_computation.7 | async-start | bytes 3538944 | tf_op jit(solution)/shard_map/reduce_scatter | solution.py:29
  263.8 170.7 %reduce-scatter.11.cloned.1.call-start = ((), (), s32[]{:S(2)}) async-start(), calls=%async_computation.11 | async-start | bytes 3538944 | tf_op jit(solution)/shard_map/reduce_scatter | solution.py:29
  294.5 1.9 copy-start.1
  311.5 24.8 %copy-start = (bf16[512,3072]{1,0:T(8,128)(2,1)S(1)}, bf16[512,3072]{1,0:T(8,128)(2,1)}, u32[]{:S(2)}) copy-start(bf16[512,3072]{1,0:T(8,128)(2,1)} %all-gather.9.cloned.1.call-done) | copy-start | bytes 9437188
Sparse Core Ops, SparseCore 0:
  10.2 63.1 all-gather.8
  75.5 59.0 all-gather.4
  137.8 36.5 reduce-scatter.8
  177.5 37.9 reduce-scatter.4
  219.4 28.5 all-gather.6
  249.9 28.5 all-gather.10
  282.7 74.2 reduce-scatter.6
  361.1 73.3 reduce-scatter.10
where the time goes:
time: 442 us; the launch traced here: 441 us
  waiting for transfers between devices  303 us (69%)
  matrix products  93.5 us (21%)
  local copies, waits for them, and re-layouts  26.7 us (6%)
  between operations  14.1 us (3%)
    all_gather x2, waiting for transfers between devices, col_panel(): return lax.all_gather(values, 'col', axis=0, tiled=True)  110 us
    dot_general x6, matrix products, contract(): lax.dot_general(left, right, ((dims[0], dims[1]), ((), ())), preferred_el...  93.5 us
    reduce_scatter x2, waiting for transfers between devices, col_sums(): lax.psum_scatter(contract(lax.dynamic_slice_in_dim(left, jnp.int32(0), le...  83.2 us
    reduce_scatter x2, waiting for transfers between devices, row_sums(): lax.psum_scatter(contract(left, right, dims).astype(jnp.bfloat16), 'row',...  65 us
    all_gather x2, waiting for transfers between devices, row_spread(): return lax.all_gather(values, 'row', axis=0, tiled=True)  42.5 us
    unnamed x5, local copies, waits for them, and re-layouts  26.7 us
  transfers between devices with their start and end apart: 8, of which 8 were waited for; matrix products, arithmetic and copies ran while one was open for 27% of the time, Pallas kernels for 0%

commit v1 on v0

--- a/solution.py
+++ b/solution.py
@@ -3,6 +3,22 @@
 import jax.numpy as jnp
 from jax import lax
 from jax.sharding import PartitionSpec as P
+
+
+def ring_gather(x, axis, dim):
+    ways, here, step = (lax.axis_size(axis), lax.axis_index(axis), x.shape[dim])
+    shape = [n * ways if d == dim else n for d, n in enumerate(x.shape)]
+    full = lax.dynamic_update_slice_in_dim(jnp.zeros(shape, x.dtype), x, here * step, axis=dim)
+    going_up = going_down = x
+    for far in range(1, ways // 2 + 1):
+        going_up = lax.ppermute(going_up, axis, [(d, (d + 1) % ways) for d in range(ways)])
+        full = lax.dynamic_update_slice_in_dim(full, going_up, (here - far) % ways * step, axis=dim)
+        if 2 * far < ways:
+            going_down = lax.ppermute(going_down, axis, [(d, (d - 1) % ways) for d in range(ways)])
+            full = lax.dynamic_update_slice_in_dim(
+                full, going_down, (here + far) % ways * step, axis=dim
+            )
+    return full
 
 
 def col_panel(values):
@@ -22,7 +38,7 @@
 
 
 def row_spread(values):
-    return lax.all_gather(values, "row", axis=0, tiled=True)
+    return ring_gather(values, "row", 0)
 
 
 def col_sums(left, right, dims):

time: 442 us -> 399 us (0.903)
  waiting for transfers between devices: 303 us -> 253 us
  local copies, waits for them, and re-layouts: 26.7 us -> 31.9 us
    ppermute x0 -> x6, waiting for transfers between devices: none -> 72.3 us  [the longest x4 72.3 us: ring_gather(): lax.ppermute(going_up, axis, [(d, (d + 1) % ways) for d in range(ways)])]
    all_gather x2 -> x0, waiting for transfers between devices: 42.5 us -> none  [row_spread(): return lax.all_gather(values, 'row', axis=0, tiled=True)]
    reduce_scatter x2, waiting for transfers between devices: 65 us -> 23.8 us  [row_sums(): lax.psum_scatter(contract(left, right, dims).astype(jnp.bfloat16), 'row',...]
    reduce_scatter x2, waiting for transfers between devices: 83.2 us -> 45.1 us  [col_sums(): lax.psum_scatter(contract(lax.dynamic_slice_in_dim(left, jnp.int32(0), le...]
    unnamed x5 -> x13, local copies, waits for them, and re-layouts: 26.7 us -> 30.7 us
  transfers between devices with their start and end apart: 8 -> 12, of which waited for: 8 -> 8; matrix products, arithmetic and copies ran while one was open for 27% -> 30% of each run, Pallas kernels for 0% -> 0%
where the time goes in v1:
time: 399 us; the launch traced here: 398 us
  waiting for transfers between devices  253 us (63%)
  matrix products  92 us (23%)
  local copies, waits for them, and re-layouts  31.9 us (8%)
  between operations  14.3 us (4%)
    all_gather x2, waiting for transfers between devices, col_panel(): return lax.all_gather(values, 'col', axis=0, tiled=True)  110 us
    dot_general x6, matrix products, contract(): lax.dot_general(left, right, ((dims[0], dims[1]), ((), ())), preferred_el...  92 us
    ppermute x4, waiting for transfers between devices, ring_gather(): lax.ppermute(going_up, axis, [(d, (d + 1) % ways) for d in range(ways)])  72.3 us
    reduce_scatter x2, waiting for transfers between devices, col_sums(): lax.psum_scatter(contract(lax.dynamic_slice_in_dim(left, jnp.int32(0), le...  45.1 us
    unnamed x13, local copies, waits for them, and re-layouts  30.7 us
    reduce_scatter x2, waiting for transfers between devices, row_sums(): lax.psum_scatter(contract(left, right, dims).astype(jnp.bfloat16), 'row',...  23.8 us
  transfers between devices with their start and end apart: 12, of which 8 were waited for; matrix products, arithmetic and copies ran while one was open for 30% of the time, Pallas kernels for 0%

profile of v1, /device:TPU:0, one launch (start us, length us, event | category | flops | bytes accessed | tf_op | source)
XLA Modules:
  0.0 398.3 jit_solution(5835694062178043810)
XLA Ops:
  7.2 0.7 all-gather.3.cloned.1.call-update
  7.9 0.7 all-gather.5.cloned.1.call-update
  8.7 64.7 %all-gather.3.cloned.1.call-done = bf16[512,3072]{1,0:T(8,128)(2,1)} async-done(((bf16[64,3072]{1,0:T(8,128)(2,1)}), bf16[512,3072]{1,0:T(8,128)(2,1)}) %all-gather.3.cloned.1.call-update) | async-done | bytes 3145744 | tf_op jit(solution)/shard_map/all_gather | solution.py:25
  73.4 15.8 %convolution_convert_fusion.4 = bf16[512,3072]{1,0:T(8,128)(2,1)} fusion(bf16[512,3072]{1,0:T(8,128)(2,1)} %all-gather.3.cloned.1.call-done, bf16[3072,3072]{1,0:T(8,128)(2,1)} %param.6), kind=kOutput, calls=%fused_computation.5 | convolution fusion | flops 9665249280 | bytes 25165824 | tf_op jit(solution)/shard_map/dot_general | solution.py:29
  89.2 45.4 %all-gather.5.cloned.1.call-done = bf16[512,3072]{1,0:T(8,128)(2,1)} async-done(((bf16[64,3072]{1,0:T(8,128)(2,1)}), bf16[512,3072]{1,0:T(8,128)(2,1)}) %all-gather.5.cloned.1.call-update) | async-done | bytes 3145744 | tf_op jit(solution)/shard_map/all_gather | solution.py:25
  134.7 15.9 %convolution_convert_fusion.2 = bf16[512,3072]{1,0:T(8,128)(2,1)} fusion(bf16[512,3072]{1,0:T(8,128)(2,1)} %all-gather.5.cloned.1.call-done, bf16[3072,3072]{1,0:T(8,128)(2,1)} %param.7), kind=kOutput, calls=%fused_computation.3 | convolution fusion | flops 9665249280 | bytes 25165824 | tf_op jit(solution)/shard_map/dot_general | solution.py:29
  150.6 23.8 %reduce-scatter.5.cloned.1.call-done = bf16[128,3072]{1,0:T(8,128)(2,1)} async-done(((bf16[512,3072]{1,0:T(8,128)(2,1)}), bf16[128,3072]{1,0:T(8,128)(2,1)}) %reduce-scatter.5.cloned.1.call-update) | async-done | bytes 786448 | tf_op jit(solution)/shard_map/reduce_scatter | solution.py:35
  174.4 1.7 fusion.8
  176.3 1.7 collective-permute-start.1
  177.9 17.5 %collective-permute-done = bf16[128,3072]{1,0:T(8,128)(2,1)S(1)} collective-permute-done((bf16[128,3072]{1,0:T(8,128)(2,1)S(1)}, bf16[128,3072]{1,0:T(8,128)(2,1)S(1)}, u32[]{:S(2)}, u32[]{:S(2)}) %collective-permute-start) | collective-permute-done | bytes 786464 | tf_op jit(solution)/shard_map/ppermute | solution.py:14
  195.5 0.4 broadcast.19.clone
  195.9 0.6 constant_dynamic-update-slice_fusion.7
  196.5 0.1 constant_dynamic-update-slice_fusion.6
  196.6 0.1 constant_dynamic-update-slice_fusion.5
  196.6 26.0 %collective-permute-done.2 = bf16[128,3072]{1,0:T(8,128)(2,1)S(1)} collective-permute-done((bf16[128,3072]{1,0:T(8,128)(2,1)S(1)}, bf16[128,3072]{1,0:T(8,128)(2,1)S(1)}, u32[]{:S(2)}, u32[]{:S(2)}) %collective-permute-start.2) | collective-permute-done | bytes 786464 | tf_op jit(solution)/shard_map/ppermute | solution.py:14
  222.7 1.6 copy-done.3
  224.4 15.0 %convolution_convert_fusion.3 = bf16[512,3072]{1,0:T(8,128)(2,1)} fusion(bf16[512,3072]{1,0:T(8,128)(2,1)S(1)} %constant_dynamic-update-slice_fusion.4, bf16[3072,3072]{1,0:T(8,128)(2,1)} %param.7), kind=kOutput, calls=%fused_computation.4 | convolution fusion | flops 9665249280 | bytes 25165824 | tf_op jit(solution)/shard_map/dot_general | solution.py:29
  239.5 0.4 broadcast.19.clone.1
  239.9 0.7 copy-done.5
  240.6 1.2 constant_dynamic-update-slice_fusion.3
  241.9 1.7 collective-permute-start.4
  243.6 17.5 %collective-permute-done.3 = bf16[128,3072]{1,0:T(8,128)(2,1)S(1)} collective-permute-done((bf16[128,3072]{1,0:T(8,128)(2,1)S(1)}, bf16[128,3072]{1,0:T(8,128)(2,1)S(1)}, u32[]{:S(2)}, u32[]{:S(2)}) %collective-permute-start.3) | collective-permute-done | bytes 786464 | tf_op jit(solution)/shard_map/ppermute | solution.py:14
  261.1 0.1 constant_dynamic-update-slice_fusion.2
  261.2 0.1 constant_dynamic-update-slice_fusion.1
  261.3 11.2 %collective-permute-done.5 = bf16[128,3072]{1,0:T(8,128)(2,1)S(1)} collective-permute-done((bf16[128,3072]{1,0:T(8,128)(2,1)S(1)}, bf16[128,3072]{1,0:T(8,128)(2,1)S(1)}, u32[]{:S(2)}, u32[]{:S(2)}) %collective-permute-start.5) | collective-permute-done | bytes 786464 | tf_op jit(solution)/shard_map/ppermute | solution.py:14
  272.6 1.7 copy-done.1
  274.3 15.2 %convolution_convert_fusion.1 = bf16[512,3072]{1,0:T(8,128)(2,1)} fusion(bf16[512,3072]{1,0:T(8,128)(2,1)S(1)} %constant_dynamic-update-slice_fusion, bf16[3072,3072]{1,0:T(8,128)(2,1)} %param.6), kind=kOutput, calls=%fused_computation.2 | convolution fusion | flops 9665249280 | bytes 25165824 | tf_op jit(solution)/shard_map/dot_general | solution.py:29
  289.5 1.9 copy-done.2
  291.4 15.0 %convert_bitcast_fusion = bf16[3072,3072]{0,1:T(8,128)(2,1)} fusion(bf16[512,3072]{1,0:T(8,128)(2,1)S(1)} %copy-done.2, bf16[512,3072]{1,0:T(8,128)(2,1)} %all-gather.3.cloned.1.call-done), kind=kOutput, calls=%fused_computation | convolution fusion | flops 9673113600 | bytes 25165824 | tf_op jit(solution)/shard_map/dot_general | solution.py:29
  306.5 24.8 %copy.8 = bf16[3072,3072]{1,0:T(8,128)(2,1)} copy(bf16[3072,3072]{0,1:T(8,128)(2,1)} %convert_bitcast_fusion) | data formatting | bytes 37748736
  331.2 15.1 %convolution_convert_fusion = bf16[3072,3072]{1,0:T(8,128)(2,1)} fusion(bf16[512,3072]{1,0:T(8,128)(2,1)S(1)} %copy-done.4, bf16[512,3072]{1,0:T(8,128)(2,1)} %all-gather.5.cloned.1.call-done), kind=kOutput, calls=%fused_computation.1 | convolution fusion | flops 9673113600 | bytes 25165824 | tf_op jit(solution)/shard_map/dot_general | solution.py:29
  346.3 45.1 %reduce-scatter.11.cloned.1.call-done = bf16[64,3072]{1,0:T(8,128)(2,1)} async-done(((bf16[512,3072]{1,0:T(8,128)(2,1)}), bf16[64,3072]{1,0:T(8,128)(2,1)}) %reduce-scatter.11.cloned.1.call-update) | async-done | bytes 393232 | tf_op jit(solution)/shard_map/reduce_scatter | solution.py:45
  (28 shorter events, 0.6 us)
Async XLA Ops:
  7.2 66.2 %all-gather.3.cloned.1.call-start = ((), (), s32[]{:S(2)}) async-start(), calls=%async_computation.4 | async-start | bytes 3538944 | tf_op jit(solution)/shard_map/all_gather | solution.py:25
  7.9 126.8 %all-gather.5.cloned.1.call-start = ((), (), s32[]{:S(2)}) async-start(), calls=%async_computation.7 | async-start | bytes 3538944 | tf_op jit(solution)/shard_map/all_gather | solution.py:25
  8.6 165.7 %reduce-scatter.5.cloned.1.call-start = ((), (), s32[]{:S(2)}) async-start(), calls=%async_computation.5 | async-start | bytes 3932160 | tf_op jit(solution)/shard_map/reduce_scatter | solution.py:35
  89.2 150.3 %reduce-scatter.9.cloned.1.call-start = ((), (), s32[]{:S(2)}) async-start(), calls=%async_computation.8 | async-start | bytes 3932160 | tf_op jit(solution)/shard_map/reduce_scatter | solution.py:35
  150.5 195.8 %reduce-scatter.7.cloned.1.call-start = ((), (), s32[]{:S(2)}) async-start(), calls=%async_computation.6 | async-start | bytes 3538944 | tf_op jit(solution)/shard_map/reduce_scatter | solution.py:45
  174.4 21.5 %copy-start = (bf16[128,3072]{1,0:T(8,128)(2,1)S(1)}, bf16[128,3072]{1,0:T(8,128)(2,1)}, u32[]{:S(2)}) copy-start(bf16[128,3072]{1,0:T(8,128)(2,1)} %reduce-scatter.5.cloned.1.call-done) | copy-start | bytes 2359300
  176.1 19.3 %collective-permute-start = (bf16[128,3072]{1,0:T(8,128)(2,1)S(1)}, bf16[128,3072]{1,0:T(8,128)(2,1)S(1)}, u32[]{:S(2)}, u32[]{:S(2)}) collective-permute-start(bf16[128,3072]{1,0:T(8,128)(2,1)S(1)} %fusion.8), channel_id=1, source_target_pairs={{0,8},{8,16},{16,24},{24,0},{1,9},{9,17},{17,25},{25,1},{2,10},{10... | collective-permute-start | bytes 2359304 | tf_op jit(solution)/shard_map/ppermute | solution.py:14
  176.3 20.3 %collective-permute-start.1 = (bf16[128,3072]{1,0:T(8,128)(2,1)S(1)}, bf16[128,3072]{1,0:T(8,128)(2,1)S(1)}, u32[]{:S(2)}, u32[]{:S(2)}) collective-permute-start(bf16[128,3072]{1,0:T(8,128)(2,1)S(1)} %fusion.8), channel_id=1, source_target_pairs={{0,24},{8,0},{16,8},{24,16},{1,25},{9,1},{17,9},{25,17},{2,26},{10... | collective-permute-start | bytes 2359304 | tf_op jit(solution)/shard_map/ppermute | solution.py:17
  195.5 27.2 %collective-permute-start.2 = (bf16[128,3072]{1,0:T(8,128)(2,1)S(1)}, bf16[128,3072]{1,0:T(8,128)(2,1)S(1)}, u32[]{:S(2)}, u32[]{:S(2)}) collective-permute-start(bf16[128,3072]{1,0:T(8,128)(2,1)S(1)} %collective-permute-done), channel_id=1, source_target_pairs={{0,8},{8,16},{16,24},{24,0},{1,9},{9,17},{17,25},{25,1},{2,10},{10... | collective-permute-start | bytes 2359304 | tf_op jit(solution)/shard_map/ppermute | solution.py:14
  222.7 1.6 copy-start.3
  239.4 152.0 %reduce-scatter.11.cloned.1.call-start = ((), (), s32[]{:S(2)}) async-start(), calls=%async_computation.9 | async-start | bytes 3538944 | tf_op jit(solution)/shard_map/reduce_scatter | solution.py:45
  239.5 1.1 copy-start.5
  241.8 19.3 %collective-permute-start.3 = (bf16[128,3072]{1,0:T(8,128)(2,1)S(1)}, bf16[128,3072]{1,0:T(8,128)(2,1)S(1)}, u32[]{:S(2)}, u32[]{:S(2)}) collective-permute-start(bf16[128,3072]{1,0:T(8,128)(2,1)S(1)} %get-tuple-element.9), channel_id=1, source_target_pairs={{0,8},{8,16},{16,24},{24,0},{1,9},{9,17},{17,25},{25,1},{2,10},{10... | collective-permute-start | bytes 2359304 | tf_op jit(solution)/shard_map/ppermute | solution.py:14
  241.9 19.3 %collective-permute-start.4 = (bf16[128,3072]{1,0:T(8,128)(2,1)S(1)}, bf16[128,3072]{1,0:T(8,128)(2,1)S(1)}, u32[]{:S(2)}, u32[]{:S(2)}) collective-permute-start(bf16[128,3072]{1,0:T(8,128)(2,1)S(1)} %get-tuple-element.9), channel_id=1, source_target_pairs={{0,24},{8,0},{16,8},{24,16},{1,25},{9,1},{17,9},{25,17},{2,26},{10... | collective-permute-start | bytes 2359304 | tf_op jit(solution)/shard_map/ppermute | solution.py:17
  261.1 11.4 %collective-permute-start.5 = (bf16[128,3072]{1,0:T(8,128)(2,1)S(1)}, bf16[128,3072]{1,0:T(8,128)(2,1)S(1)}, u32[]{:S(2)}, u32[]{:S(2)}) collective-permute-start(bf16[128,3072]{1,0:T(8,128)(2,1)S(1)} %collective-permute-done.3), channel_id=1, source_target_pairs={{0,8},{8,16},{16,24},{24,0},{1,9},{9,17},{17,25},{25,1},{2,10},{10... | collective-permute-start | bytes 2359304 | tf_op jit(solution)/shard_map/ppermute | solution.py:14
  272.6 1.7 copy-start.1
  289.5 1.9 copy-start.2
  306.5 24.8 %copy-start.4 = (bf16[512,3072]{1,0:T(8,128)(2,1)S(1)}, bf16[512,3072]{1,0:T(8,128)(2,1)}, u32[]{:S(2)}) copy-start(bf16[512,3072]{1,0:T(8,128)(2,1)} %copy-done.3) | copy-start | bytes 9437188
Sparse Core Ops, SparseCore 0:
  10.2 63.1 all-gather.2
  75.5 59.0 all-gather.4
  137.8 36.5 reduce-scatter.4
  177.5 46.0 reduce-scatter.8
  239.6 74.3 reduce-scatter.6
  317.9 73.4 reduce-scatter.10
